TPU v7x, 32 devices: a whole 2x2x4 slice. The times are simulated.
32 devices in a mesh: groups: 2 (over y), vocab: 4 (over z), edit: 2 (over x), tok: 2 (over core).
Axes of the slice: x: 2, y: 2, z: 4, core: 2. Of those that a mesh axis runs over, the one named last changes fastest.
Arguments:
- token_ids: int32 [256], P(('groups', 'tok')), parts along dimension 0, may hold values from 0 to 4095
- valid_mask: int32 [256], P(('groups', 'tok')), parts along dimension 0, may hold values 0 or 1
- key_index: int32 [4], P('groups'), parts along dimension 0, may hold values from 0 to 3
- hidden_act: bfloat16 [256, 14336], P(('groups', 'tok'), 'vocab'), parts along dimension 0, may hold values from -6 to 6
- key_table: bfloat16 [4, 14336], P(None, 'vocab'), may hold values from -0.046875 to 0.046875
- base_out: bfloat16 [256, 4096], P(('groups', 'tok'), 'vocab'), parts along dimension 0, may hold values from -50 to 50
- value_vecs: bfloat16 [4, 4096], P(('groups', 'edit'), 'vocab'), parts along dimension 0, may hold values from -6 to 6
- norm_gain: float32 [4096], replicated, may hold values from 0.5 to 1.5
- head: bfloat16 [4096, 4096], P(('vocab', 'edit')), may hold values from -46 to 46
Outputs:
- grad_value: float32 [4, 4096], P(('groups', 'edit'), 'vocab'), parts along dimension 0
- token_kl: float32 [4, 128], P(('groups', 'edit'), 'tok'), parts along dimension 0
- target_logprob: float32 [4, 128], P(('groups', 'edit'), 'tok'), parts along dimension 0
There are 2 independent parts, one for each index of `groups`. A program takes and returns all parts, laid end to end along the dimension named above; an argument that names none is the same for every part. Nothing has to cross between parts.
All inputs are finite; a program needn't handle non-finite values. No bound on the sum of `valid_mask` on one device may be relied on, other than what follows from the above.
Results may differ from a plain program's by a relative error of at most 0.0061.
Values may be sent and summed in bfloat16 or wider, within the bound.
A program may use at most 64 MiB of HBM per device.

v0:
```python
import jax
import jax.numpy as jnp
from jax import lax
from jax.sharding import PartitionSpec as P

NORM_EPS = 1e-05


def rms_scale(hidden_rows):
    return lax.rsqrt(jnp.mean(hidden_rows * hidden_rows, axis=-1, keepdims=True) + NORM_EPS)


def per_device(
    token_ids, valid_mask, key_index, hidden_act, key_table, base_out, value_vecs, norm_gain, head
):
    vocab_rows = head.shape[0]
    edit_rows = value_vecs.shape[0]
    piece_width = value_vecs.shape[1]
    key_slots = jnp.arange(key_table.shape[0], dtype=jnp.int32)
    select = (key_index[:, None] == key_slots[None, :]).astype(jnp.bfloat16)
    edit_keys = jnp.dot(select, key_table, preferred_element_type=jnp.float32).astype(jnp.bfloat16)
    coeff_part = lax.dot_general(
        edit_keys, hidden_act, (((1,), (1,)), ((), ())), preferred_element_type=jnp.float32
    )
    coeff = lax.psum(coeff_part, "vocab")
    base_rows, local_values = (
        lax.all_gather(base_out, "vocab", axis=1, tiled=True),
        lax.all_gather(value_vecs, "vocab", axis=1, tiled=True),
    )
    values = lax.all_gather(local_values, "edit", axis=0, tiled=True)
    base32 = base_rows.astype(jnp.float32)
    base_norm = (norm_gain * base32 * rms_scale(base32)).astype(jnp.bfloat16)
    base_logits = lax.dot_general(
        base_norm, head, (((1,), (1,)), ((), ())), preferred_element_type=jnp.float32
    )
    edited = base32[None, :, :] + coeff[:, :, None] * values.astype(jnp.float32)[:, None, :]
    row_scale = rms_scale(edited)
    normed = (norm_gain * edited * row_scale).astype(jnp.bfloat16)
    logits = jnp.einsum("etd,vd->etv", normed, head, preferred_element_type=jnp.float32)
    vocab_start = lax.axis_index(("vocab", "edit")) * vocab_rows
    vocab_ids = vocab_start + jnp.arange(vocab_rows, dtype=jnp.int32)
    onehot = (token_ids[:, None] == vocab_ids[None, :]).astype(jnp.float32)
    peak_base = jnp.max(base_logits, axis=-1)
    peak_edit = jnp.max(logits, axis=-1)
    peak_base, peak_edit = lax.pmax((peak_base, peak_edit), ("vocab", "edit"))
    base_exp = jnp.exp(base_logits - peak_base[:, None])
    base_total = jnp.sum(base_exp, axis=-1)
    edit_total = jnp.sum(jnp.exp(logits - peak_edit[:, :, None]), axis=-1)
    cross_sum = jnp.sum(base_exp[None, :, :] * (base_logits[None, :, :] - logits), axis=-1)
    target = jnp.sum(onehot[None, :, :] * logits, axis=-1)
    base_total, edit_total, cross_sum, target = lax.psum(
        (base_total, edit_total, cross_sum, target), ("vocab", "edit")
    )
    base_lse = peak_base + jnp.log(base_total)
    edit_lse = peak_edit + jnp.log(edit_total)
    valid = valid_mask.astype(jnp.float32)
    token_kl = valid[None, :] * (cross_sum / base_total[None, :] - base_lse[None, :] + edit_lse)
    target_logprob = target - edit_lse
    base_prob = jnp.exp(base_logits - base_lse[:, None])
    edit_prob = jnp.exp(logits - edit_lse[:, :, None])
    logit_grad = (valid[None, :, None] * (edit_prob - base_prob[None, :, :])).astype(jnp.bfloat16)
    back_rows = jnp.einsum("etv,vd->etd", logit_grad, head, preferred_element_type=jnp.float32)
    grad_y = norm_gain * back_rows
    grad_o = row_scale * grad_y - edited * row_scale**3 * jnp.mean(
        grad_y * edited, axis=-1, keepdims=True
    )
    grad_part = jnp.sum(coeff[:, :, None] * grad_o, axis=1)
    edit_start = lax.axis_index("edit") * edit_rows
    grad_total = lax.psum(grad_part, ("vocab", "edit", "tok"))
    grad_mine = lax.dynamic_slice_in_dim(grad_total, edit_start, edit_rows, 0)
    grad_piece = lax.dynamic_slice_in_dim(
        grad_mine, lax.axis_index("vocab") * piece_width, piece_width, 1
    )
    kl_mine = lax.dynamic_slice_in_dim(token_kl, edit_start, edit_rows, 0)
    target_mine = lax.dynamic_slice_in_dim(target_logprob, edit_start, edit_rows, 0)
    return (grad_piece, kl_mine, target_mine)


def solution(mesh):
    placed = (
        P(("groups", "tok")),
        P(("groups", "tok")),
        P("groups"),
        P(("groups", "tok"), "vocab"),
        P(None, "vocab"),
        P(("groups", "tok"), "vocab"),
        P(("groups", "edit"), "vocab"),
        P(),
        P(("vocab", "edit"), None),
    )
    return jax.shard_map(
        per_device,
        mesh=mesh,
        in_specs=placed,
        out_specs=(
            P(("groups", "edit"), "vocab"),
            P(("groups", "edit"), "tok"),
            P(("groups", "edit"), "tok"),
        ),
        check_vma=False,
    )
```

profile of v0, /device:TPU:0, one launch (start us, length us, event | category | flops | bytes accessed | tf_op | source)
XLA Modules:
  0.0 156.0 jit_solution(18408327459742363050)
XLA Ops:
  0.6 0.0 copy-start
  0.7 0.7 convert_element_type.32
  1.4 0.3 copy-done
  1.7 1.1 fusion.3
  2.8 13.4 %psum.42 = f32[2,64]{1,0:T(2,128)S(1)} all-reduce(f32[2,64]{1,0:T(2,128)S(1)} %fusion.3), channel_id=1, replica_groups=mesh['groups'=2,'vocab'=4,'edit'=2,'tok'=2] {'vocab'}, use_global_device_ids=true, to_apply=%region_0.0 | all-reduce | flops 128 | bytes 1024 | tf_op jit(solution)/shard_map/psum | solution.py:25
  16.3 13.3 %all_gather.10 = bf16[1,4096]{1,0:T(2,128)(2,1)S(1)} all-gather(bf16[1,1024]{1,0:T(2,128)(2,1)} %param.15), channel_id=1, replica_groups=mesh['groups'=2,'vocab'=4,'edit'=2,'tok'=2] {'vocab'}, dimensions={1}, use_global_device_ids=true | all-gather | bytes 10240 | tf_op jit(solution)/shard_map/all_gather | solution.py:28
  29.5 4.4 %all-gather = bf16[2,1,4096]{2,1,0:T(2,128)(2,1)S(1)} all-gather(bf16[1,1,4096]{2,1,0:T(2,128)(2,1)S(1)} %bitcast.20), channel_id=1, replica_groups=mesh['groups'=2,'vocab'=4,'edit'=2,'tok'=2] {'edit'}, dimensions={0}, use_global_device_ids=true | all-gather | bytes 24576 | tf_op jit(solution)/shard_map/all_gather | solution.py:30
  34.0 0.7 compare_convert_fusion
  34.7 15.0 %all_gather.9 = bf16[64,4096]{1,0:T(8,128)(2,1)S(1)} all-gather(bf16[64,1024]{1,0:T(8,128)(2,1)} %param.14), channel_id=1, replica_groups=mesh['groups'=2,'vocab'=4,'edit'=2,'tok'=2] {'vocab'}, dimensions={1}, use_global_device_ids=true | all-gather | bytes 655360 | tf_op jit(solution)/shard_map/all_gather | solution.py:27
  49.7 0.2 multiply_reduce_fusion.3
  49.9 0.0 copy-start.1
  49.9 3.9 %fusion.24 = (f32[64]{0:T(128)S(1)}, f32[64,512]{1,0:T(8,128)S(1)}) fusion(bf16[512,4096]{1,0:T(8,128)(2,1)} %param.17, f32[64]{0:T(128)S(1)} %add_rsqrt_fusion.1, f32[4096]{0:T(1024)} %param.16, bf16[64,4096]{1,0:T(8,128)(2,1)S(1)} %all_gather.9), kind=kOutput, calls=%fused_computation.48 | convolution fusion | flops 269516736 | bytes 4866560 | tf_op jit(solution)/shard_map/dot_general | solution.py:33
  53.8 0.0 copy-start.2
  53.8 0.1 convert_element_type.30
  53.9 0.4 multiply_reduce_fusion.2
  54.3 0.0 copy-done.1
  54.3 0.2 copy-done.2
  54.5 1.6 %fusion.25 = (f32[2,64]{1,0:T(2,128)S(1)}, f32[2,64,512]{2,1,0:T(8,128)S(1)}) fusion(bf16[512,4096]{1,0:T(8,128)(2,1)S(1)} %copy-done.1, f32[4096]{0:T(1024)S(1)} %copy-done.2, f32[2,64]{1,0:T(2,128)S(1)} %get-tuple-element.17, f32[2,4096]{1,0:T(2,128)S(1)} %bitcast.17, f32[64,4096]{1,0:T(8,128)S(1)} %convert_element_type.30, f32[2,64]{1,0:T(2,128)S(1)} %psum.42), kind=kOutput, calls=%fused_computation.49 | convolution fusion | flops 539557760 | bytes 5555712 | tf_op jit(solution)/shard_map/etd,vd->etv/dot_general | solution.py:39
  56.1 18.6 %all-reduce.1 = (f32[64]{0:T(128)S(1)}, f32[2,64]{1,0:T(2,128)S(1)}) all-reduce(f32[64]{0:T(128)S(1)} %get-tuple-element.18, f32[2,64]{1,0:T(2,128)S(1)} %get-tuple-element.20), channel_id=1, replica_groups=mesh['groups'=2,'vocab'=4,'edit'=2,'tok'=2] {'vocab','edit'}, use_global_device_ids=true, to_apply=%region_8.0 | all-reduce | flops 192 | bytes 1536 | tf_op jit(solution)/shard_map/pmax | solution.py:45
  74.7 0.2 fusion.23
  74.9 0.2 multiply_reduce_fusion.4
  75.1 17.7 %all-reduce = (f32[64]{0:T(128)S(1)}, f32[2,64]{1,0:T(2,128)S(1)}, f32[2,64]{1,0:T(2,128)S(1)}, f32[2,64]{1,0:T(2,128)S(1)}) all-reduce(f32[64]{0:T(128)S(1)} %get-tuple-element.14, f32[2,64]{1,0:T(2,128)S(1)} %get-tuple-element.5, ...), channel_id=1, replica_groups=mesh['groups'=2,'vocab'=4,'edit'=2,'tok'=2] {'vocab','edit'}, use_global_device_ids=true, to_apply=%region_10.0 | all-reduce | flops 448 | bytes 3584 | tf_op jit(solution)/shard_map/psum | solution.py:51
  92.8 0.1 subtract_exponential_fusion
  92.9 0.5 constant_dynamic-slice_fusion
  93.4 3.4 %multiply_reduce_fusion.1 = (f32[2,64]{1,0:T(2,128)S(1)}, f32[2,64,4096]{2,1,0:T(8,128)S(1)}) fusion(f32[2,4096]{1,0:T(2,128)S(1)} %bitcast.18, f32[64,4096]{1,0:T(8,128)S(1)} %convert_element_type.30, f32[2,64]{1,0:T(2,128)S(1)} %psum.42, bf16[512,4096]{1,0:T(8,128)(2,1)} %param.17, f32[2,64,512]{2,1,0:T(8,128)S(1)} %get-tuple-element.21, ...), kind=kOutput, calls=%fused_computation.6 | convolution fusion | flops 539754368 | bytes 7784192 | tf_op jit(solution)/shard_map/etv,vd->etd/dot_general | solution.py:62
  96.9 0.8 multiply_reduce_fusion
  97.7 57.6 %psum.45 = f32[2,4096]{1,0:T(2,128)S(1)} all-reduce(f32[2,4096]{1,0:T(2,128)S(1)} %multiply_reduce_fusion), channel_id=1, replica_groups=mesh['groups'=2,'vocab'=4,'edit'=2,'tok'=2] {'vocab','edit','tok'}, use_global_device_ids=true, to_apply=%region_13.0 | all-reduce | flops 8192 | bytes 65536 | tf_op jit(solution)/shard_map/psum | solution.py:69
  155.3 0.7 dynamic_slice.10
  (8 shorter events, 0.1 us)
Async XLA Ops:
  0.6 1.0 copy-start
  49.9 4.4 %copy-start.1 = (bf16[512,4096]{1,0:T(8,128)(2,1)S(1)}, bf16[512,4096]{1,0:T(8,128)(2,1)}, u32[]{:S(2)}) copy-start(bf16[512,4096]{1,0:T(8,128)(2,1)} %param.17) | copy-start | bytes 12582916
  53.8 0.7 copy-start.2
where the time goes:
time: 156 us
  blocking collectives  140 us (90%)
  matrix products  10 us (6%)
  other arithmetic  3.51 us (2%)
  local copies, waits for them, and re-layouts  1.73 us (1%)
    psum x1, blocking collectives, per_device(): grad_total = lax.psum(grad_part, ('vocab', 'edit', 'tok'))  57.6 us
    pmax x1, blocking collectives, per_device(): peak_base, peak_edit = lax.pmax((peak_base, peak_edit), ('vocab', 'edit'))  18.6 us
    psum x1, blocking collectives, per_device(): lax.psum((base_total, edit_total, cross_sum, target), ('vocab', 'edit'))  17.7 us
    all_gather x1, blocking collectives, per_device(): lax.all_gather(base_out, 'vocab', axis=1, tiled=True)  15 us
    psum x1, blocking collectives, per_device(): coeff = lax.psum(coeff_part, 'vocab')  13.4 us
    all_gather x1, blocking collectives, per_device(): lax.all_gather(value_vecs, 'vocab', axis=1, tiled=True)  13.3 us
    all_gather x1, blocking collectives, per_device(): values = lax.all_gather(local_values, 'edit', axis=0, tiled=True)  4.4 us
    dot_general x1, matrix products, per_device(): lax.dot_general(base_norm, head, (((1,), (1,)), ((), ())), preferred_elem...  3.87 us

commit v1 on v0

--- a/solution.py
+++ b/solution.py
@@ -4,6 +4,11 @@
 from jax.sharding import PartitionSpec as P
 
 NORM_EPS = 1e-05
+
+
+def axis_by_axis(value, one, other):
+    inner = lax.psum(value, one)
+    return lax.psum(inner, other)
 
 
 def rms_scale(hidden_rows):
@@ -48,8 +53,8 @@
     edit_total = jnp.sum(jnp.exp(logits - peak_edit[:, :, None]), axis=-1)
     cross_sum = jnp.sum(base_exp[None, :, :] * (base_logits[None, :, :] - logits), axis=-1)
     target = jnp.sum(onehot[None, :, :] * logits, axis=-1)
-    base_total, edit_total, cross_sum, target = lax.psum(
-        (base_total, edit_total, cross_sum, target), ("vocab", "edit")
+    base_total, edit_total, cross_sum, target = axis_by_axis(
+        (base_total, edit_total, cross_sum, target), "edit", "vocab"
     )
     base_lse = peak_base + jnp.log(base_total)
     edit_lse = peak_edit + jnp.log(edit_total)

time: 156 us -> 152 us (0.974)
  blocking collectives: 140 us -> 136 us
    psum x1 -> x2, blocking collectives: 17.7 us -> 13.3 us  [the longest x1 8.34 us: axis_by_axis(): return lax.psum(inner, other)]
where the time goes in v1:
time: 152 us
  blocking collectives  136 us (89%)
  matrix products  10 us (7%)
  other arithmetic  3.51 us (2%)
  local copies, waits for them, and re-layouts  1.73 us (1%)
    psum x1, blocking collectives, per_device(): grad_total = lax.psum(grad_part, ('vocab', 'edit', 'tok'))  57.6 us
    pmax x1, blocking collectives, per_device(): peak_base, peak_edit = lax.pmax((peak_base, peak_edit), ('vocab', 'edit'))  18.6 us
    all_gather x1, blocking collectives, per_device(): lax.all_gather(base_out, 'vocab', axis=1, tiled=True)  15 us
    psum x1, blocking collectives, per_device(): coeff = lax.psum(coeff_part, 'vocab')  13.4 us
    all_gather x1, blocking collectives, per_device(): lax.all_gather(value_vecs, 'vocab', axis=1, tiled=True)  13.3 us
    psum x1, blocking collectives, axis_by_axis(): return lax.psum(inner, other)  8.34 us
    psum x1, blocking collectives, axis_by_axis(): inner = lax.psum(value, one)  4.94 us
    all_gather x1, blocking collectives, per_device(): values = lax.all_gather(local_values, 'edit', axis=0, tiled=True)  4.4 us

profile of v1, /device:TPU:0, one launch (start us, length us, event | category | flops | bytes accessed | tf_op | source)
XLA Modules:
  0.0 151.6 jit_solution(2416265030503797968)
XLA Ops:
  0.6 0.0 copy-start
  0.7 0.7 convert_element_type.32
  1.4 0.3 copy-done
  1.7 1.1 fusion.3
  2.8 13.4 %psum.70 = f32[2,64]{1,0:T(2,128)S(1)} all-reduce(f32[2,64]{1,0:T(2,128)S(1)} %fusion.3), channel_id=1, replica_groups=mesh['groups'=2,'vocab'=4,'edit'=2,'tok'=2] {'vocab'}, use_global_device_ids=true, to_apply=%region_0.0 | all-reduce | flops 128 | bytes 1024 | tf_op jit(solution)/shard_map/psum | solution.py:30
  16.3 13.3 %all_gather.10 = bf16[1,4096]{1,0:T(2,128)(2,1)S(1)} all-gather(bf16[1,1024]{1,0:T(2,128)(2,1)} %param.15), channel_id=1, replica_groups=mesh['groups'=2,'vocab'=4,'edit'=2,'tok'=2] {'vocab'}, dimensions={1}, use_global_device_ids=true | all-gather | bytes 10240 | tf_op jit(solution)/shard_map/all_gather | solution.py:33
  29.5 4.4 %all-gather = bf16[2,1,4096]{2,1,0:T(2,128)(2,1)S(1)} all-gather(bf16[1,1,4096]{2,1,0:T(2,128)(2,1)S(1)} %bitcast.20), channel_id=1, replica_groups=mesh['groups'=2,'vocab'=4,'edit'=2,'tok'=2] {'edit'}, dimensions={0}, use_global_device_ids=true | all-gather | bytes 24576 | tf_op jit(solution)/shard_map/all_gather | solution.py:35
  34.0 0.7 compare_convert_fusion
  34.7 15.0 %all_gather.9 = bf16[64,4096]{1,0:T(8,128)(2,1)S(1)} all-gather(bf16[64,1024]{1,0:T(8,128)(2,1)} %param.14), channel_id=1, replica_groups=mesh['groups'=2,'vocab'=4,'edit'=2,'tok'=2] {'vocab'}, dimensions={1}, use_global_device_ids=true | all-gather | bytes 655360 | tf_op jit(solution)/shard_map/all_gather | solution.py:32
  49.7 0.2 multiply_reduce_fusion.3
  49.9 0.0 copy-start.1
  49.9 3.9 %fusion.24 = (f32[64]{0:T(128)S(1)}, f32[64,512]{1,0:T(8,128)S(1)}) fusion(bf16[512,4096]{1,0:T(8,128)(2,1)} %param.17, f32[64]{0:T(128)S(1)} %add_rsqrt_fusion.1, f32[4096]{0:T(1024)} %param.16, bf16[64,4096]{1,0:T(8,128)(2,1)S(1)} %all_gather.9), kind=kOutput, calls=%fused_computation.48 | convolution fusion | flops 269516736 | bytes 4866560 | tf_op jit(solution)/shard_map/dot_general | solution.py:38
  53.8 0.0 copy-start.2
  53.8 0.1 convert_element_type.30
  53.9 0.4 multiply_reduce_fusion.2
  54.3 0.0 copy-done.1
  54.3 0.2 copy-done.2
  54.5 1.6 %fusion.25 = (f32[2,64]{1,0:T(2,128)S(1)}, f32[2,64,512]{2,1,0:T(8,128)S(1)}) fusion(bf16[512,4096]{1,0:T(8,128)(2,1)S(1)} %copy-done.1, f32[4096]{0:T(1024)S(1)} %copy-done.2, f32[2,64]{1,0:T(2,128)S(1)} %get-tuple-element.21, f32[2,4096]{1,0:T(2,128)S(1)} %bitcast.17, f32[64,4096]{1,0:T(8,128)S(1)} %convert_element_type.30, f32[2,64]{1,0:T(2,128)S(1)} %psum.70), kind=kOutput, calls=%fused_computation.49 | convolution fusion | flops 539557760 | bytes 5555712 | tf_op jit(solution)/shard_map/etd,vd->etv/dot_general | solution.py:44
  56.1 18.6 %all-reduce = (f32[64]{0:T(128)S(1)}, f32[2,64]{1,0:T(2,128)S(1)}) all-reduce(f32[64]{0:T(128)S(1)} %get-tuple-element.22, f32[2,64]{1,0:T(2,128)S(1)} %get-tuple-element.24), channel_id=1, replica_groups=mesh['groups'=2,'vocab'=4,'edit'=2,'tok'=2] {'vocab','edit'}, use_global_device_ids=true, to_apply=%region_9.0 | all-reduce | flops 192 | bytes 1536 | tf_op jit(solution)/shard_map/pmax | solution.py:50
  74.7 0.2 fusion.23
  74.9 0.2 multiply_reduce_fusion.4
  75.1 4.9 %all-reduce.2 = (f32[64]{0:T(128)S(1)}, f32[2,64]{1,0:T(2,128)S(1)}, f32[2,64]{1,0:T(2,128)S(1)}, f32[2,64]{1,0:T(2,128)S(1)}) all-reduce(f32[64]{0:T(128)S(1)} %get-tuple-element.18, f32[2,64]{1,0:T(2,128)S(1)} %get-tuple-element.5, ...), channel_id=1, replica_groups=mesh['groups'=2,'vocab'=4,'edit'=2,'tok'=2] {'edit'}, use_global_device_ids=true, to_apply=%region_11.0 | all-reduce | flops 448 | bytes 3584 | tf_op jit(solution)/shard_map/psum | solution.py:10
  80.1 8.3 %all-reduce.1 = (f32[64]{0:T(128)S(1)}, f32[2,64]{1,0:T(2,128)S(1)}, f32[2,64]{1,0:T(2,128)S(1)}, f32[2,64]{1,0:T(2,128)S(1)}) all-reduce(f32[64]{0:T(128)S(1)} %get-tuple-element.12, f32[2,64]{1,0:T(2,128)S(1)} %get-tuple-element.13, ...), channel_id=1, replica_groups=mesh['groups'=2,'vocab'=4,'edit'=2,'tok'=2] {'vocab'}, use_global_device_ids=true, to_apply=%region_12.0 | all-reduce | flops 448 | bytes 3584 | tf_op jit(solution)/shard_map/psum | solution.py:11
  88.4 0.1 subtract_exponential_fusion
  88.5 0.5 constant_dynamic-slice_fusion
  89.1 3.4 %multiply_reduce_fusion.1 = (f32[2,64]{1,0:T(2,128)S(1)}, f32[2,64,4096]{2,1,0:T(8,128)S(1)}) fusion(f32[2,4096]{1,0:T(2,128)S(1)} %bitcast.18, f32[64,4096]{1,0:T(8,128)S(1)} %convert_element_type.30, f32[2,64]{1,0:T(2,128)S(1)} %psum.70, bf16[512,4096]{1,0:T(8,128)(2,1)} %param.17, f32[2,64,512]{2,1,0:T(8,128)S(1)} %get-tuple-element.25, ...), kind=kOutput, calls=%fused_computation.6 | convolution fusion | flops 539754368 | bytes 7784192 | tf_op jit(solution)/shard_map/etv,vd->etd/dot_general | solution.py:67
  92.5 0.8 multiply_reduce_fusion
  93.3 57.6 %psum.75 = f32[2,4096]{1,0:T(2,128)S(1)} all-reduce(f32[2,4096]{1,0:T(2,128)S(1)} %multiply_reduce_fusion), channel_id=1, replica_groups=mesh['groups'=2,'vocab'=4,'edit'=2,'tok'=2] {'vocab','edit','tok'}, use_global_device_ids=true, to_apply=%region_15.0 | all-reduce | flops 8192 | bytes 65536 | tf_op jit(solution)/shard_map/psum | solution.py:74
  150.9 0.7 dynamic_slice.10
  (8 shorter events, 0.1 us)
Async XLA Ops:
  0.6 1.0 copy-start
  49.9 4.4 %copy-start.1 = (bf16[512,4096]{1,0:T(8,128)(2,1)S(1)}, bf16[512,4096]{1,0:T(8,128)(2,1)}, u32[]{:S(2)}) copy-start(bf16[512,4096]{1,0:T(8,128)(2,1)} %param.17) | copy-start | bytes 12582916
  53.8 0.7 copy-start.2
